TPU v7x, 32 devices: a whole 2x2x4 slice. The times are simulated.
32 devices in a mesh: rep: 16 (over z, x, core), shard: 2 (over y).
Axes of the slice: x: 2, y: 2, z: 4, core: 2. Of those that a mesh axis runs over, the one named last changes fastest.
Arguments:
- hidden_in: bfloat16 [4096, 1024], P(('rep', 'shard')), may hold values from -6 to 6
- cotangent: bfloat16 [4096, 1024], P(('rep', 'shard')), may hold values from -6 to 6
- norm_gain: float32 [1, 1024], P(None, 'shard'), may hold values from 0.5 to 1.5
- w_z: bfloat16 [1, 1024, 2048], P(None, None, 'shard'), may hold values from -0.1875 to 0.1875
- w_x: bfloat16 [1, 1024, 2048], P(None, None, 'shard'), may hold values from -0.1875 to 0.1875
- w_bc: bfloat16 [1, 1024, 256], P(None, None, 'shard'), may hold values from -0.1875 to 0.1875
- w_dt: bfloat16 [1, 1024, 32], P(None, None, 'shard'), may hold values from -0.1875 to 0.1875
- conv_x: float32 [1, 4, 2048], P(None, None, 'shard'), may hold values from -3 to 3
- conv_bc: float32 [1, 4, 256], P(None, None, 'shard'), may hold values from -3 to 3
- bias_x: float32 [1, 2048], P(None, 'shard'), may hold values from -1.75 to 1.75
- bias_bc: float32 [1, 256], P(None, 'shard'), may hold values from -1.75 to 1.75
- dt_bias: float32 [1, 32], P(None, 'shard'), may hold values from -5 to -2
- a_log: float32 [1, 32], P(None, 'shard'), may hold values from 0 to 2.77
- d_skip: float32 [1, 32], P(None, 'shard'), may hold values from 0.5 to 1.5
- gate_gain: float32 [1, 2048], P(None, 'shard'), may hold values from 0.5 to 1.5
- w_out: bfloat16 [1, 2048, 1024], P(None, 'shard'), may hold values from -0.125 to 0.125
- seq_len: int32 [256], replicated, may hold values from 0 to 128, as said below
- seq_owner: int32 [256], replicated, may hold values from 0 to 31, as said below
- seq_start: int32 [256], replicated, may hold values from 0 to 128, as said below
Outputs:
- hidden_out: float32 [4096, 1024], P(('rep', 'shard'))
- grad_hidden: float32 [4096, 1024], P(('rep', 'shard'))
- grad_norm_gain: float32 [1, 1024], P(None, 'shard')
- grad_w_z: float32 [1, 1024, 2048], P(None, None, 'shard')
- grad_w_x: float32 [1, 1024, 2048], P(None, None, 'shard')
- grad_w_bc: float32 [1, 1024, 256], P(None, None, 'shard')
- grad_w_dt: float32 [1, 1024, 32], P(None, None, 'shard')
- grad_conv_x: float32 [1, 4, 2048], P(None, None, 'shard')
- grad_conv_bc: float32 [1, 4, 256], P(None, None, 'shard')
- grad_bias_x: float32 [1, 2048], P(None, 'shard')
- grad_bias_bc: float32 [1, 256], P(None, 'shard')
- grad_dt_bias: float32 [1, 32], P(None, 'shard')
- grad_a_log: float32 [1, 32], P(None, 'shard')
- grad_d_skip: float32 [1, 32], P(None, 'shard')
- grad_gate_gain: float32 [1, 2048], P(None, 'shard')
- grad_w_out: float32 [1, 2048, 1024], P(None, 'shard')
Inputs may be any that keep to these rules, and one draw needn't show every extreme that they name: `seq_len`: the records come in groups of 8 in a row; each group belongs to exactly one device, and every device has one group. A group's sequences lie back to back from its device's first slot in record order, never past its last slot; some records are empty. `seq_owner`: all records of a group name the same device. `seq_start`: A record starts where the previous record of its group ends, the first at slot 0; an empty record may start at slot 128.
All inputs are finite; a program needn't handle non-finite values.
Results may differ from a plain program's by a relative error of at most 0.04.
Values may be sent and summed in bfloat16 or wider, within the bound.
No kernel may reach another device: no remote copies, remote signals or barrier semaphores. Data moves between devices by JAX's collectives and lax.ppermute only.
A program may use at most 128 MiB of HBM per device.

v0:
```python
from functools import partial
import jax
import jax.numpy as jnp
from jax import lax
from jax.sharding import PartitionSpec as P

BLOCK = 64
INNER = 2048
epsilon = 1e-05
HIGHEST = lax.Precision.HIGHEST


def slot_segments(seq_len, seq_owner, seq_start, device, row_count):
    slot_ids = jnp.arange(row_count, dtype=jnp.int32)
    record_ids = jnp.arange(seq_len.shape[0], dtype=jnp.int32)
    covers = (
        (seq_owner[:, None] == device)
        & (slot_ids[None, :] >= seq_start[:, None])
        & (slot_ids[None, :] < seq_start[:, None] + seq_len[:, None])
    )
    in_use = jnp.sum(covers.astype(jnp.int32), axis=0)
    covering = jnp.sum(jnp.where(covers, record_ids[:, None], 0), axis=0)
    lone_ids = seq_len.shape[0] + device * row_count + slot_ids
    segment = jnp.where(in_use > 0, covering, lone_ids)
    return (segment, in_use)


def causal_conv(inputs, kernel, bias_row, segment):
    kernel_len = kernel.shape[0]
    row_count = inputs.shape[0]
    result = bias_row[None, :] + kernel[kernel_len - 1][None, :] * inputs
    for offset in range(1, kernel_len):
        shifted = jnp.pad(inputs, ((offset, 0), (0, 0)))[:row_count]
        earlier = jnp.pad(segment, (offset, 0), constant_values=-1)[:row_count]
        same_seq = (earlier == segment).astype(inputs.dtype)
        result = result + kernel[kernel_len - 1 - offset][None, :] * shifted * same_seq[:, None]
    return result


def carry_state(state, inputs):
    local_part, span_total, keep_flag = inputs
    updated = local_part + keep_flag * jnp.exp(span_total)[:, None, None] * state
    return (updated, state)


def mixer_core(
    inner_x, inner_bc, dt_raw, conv_x, conv_bc, bias_x, bias_bc, dt_bias, a_log, d_skip, segment
):
    row_count = inner_x.shape[0]
    head_count = dt_raw.shape[1]
    head_size = inner_x.shape[1] // head_count
    state_size = inner_bc.shape[1] // 2
    bin_count = row_count // BLOCK
    values = jax.nn.silu(causal_conv(inner_x, conv_x, bias_x, segment))
    maps_both = jax.nn.silu(causal_conv(inner_bc, conv_bc, bias_bc, segment))
    step_size = jax.nn.softplus(dt_raw + dt_bias[None, :])
    log_decay = -step_size * jnp.exp(a_log)[None, :]
    cumulative = jnp.transpose(
        jnp.cumsum(log_decay.reshape(bin_count, BLOCK, head_count), axis=1), (0, 2, 1)
    )
    step_rows = jnp.transpose(step_size.reshape(bin_count, BLOCK, head_count), (0, 2, 1))
    bin_segment = segment.reshape(bin_count, BLOCK)
    positions = jnp.arange(BLOCK, dtype=jnp.int32)
    causal = (positions[:, None] >= positions[None, :])[None, :, :] & (
        bin_segment[:, :, None] == bin_segment[:, None, :]
    )
    causal = causal[:, None, :, :]
    log_gaps = cumulative[:, :, :, None] - cumulative[:, :, None, :]
    decay_rows = jnp.where(causal, jnp.exp(jnp.where(causal, log_gaps, 0.0)), 0.0)
    key_rows = maps_both[:, :state_size].reshape(bin_count, BLOCK, state_size)
    query_rows = maps_both[:, state_size:].reshape(bin_count, BLOCK, state_size)
    scores = jnp.einsum("btn,bsn->bts", query_rows, key_rows, precision=HIGHEST)
    mixing = scores[:, None, :, :] * decay_rows * step_rows[:, :, None, :]
    head_values = values.reshape(bin_count, BLOCK, head_count, head_size)
    result = jnp.einsum("bhts,bshp->bthp", mixing, head_values, precision=HIGHEST)
    span_total = cumulative[:, :, BLOCK - 1]
    last_segment = bin_segment[:, BLOCK - 1]
    prior_segment = jnp.concatenate([jnp.full((1,), -1, jnp.int32), last_segment[:-1]])
    in_last = (bin_segment == last_segment[:, None]).astype(jnp.float32)
    tail_weights = jnp.exp(span_total[:, :, None] - cumulative) * step_rows * in_last[:, None, :]
    weighted_values = head_values * jnp.transpose(tail_weights, (0, 2, 1))[:, :, :, None]
    local_states = jnp.einsum("bshp,bsn->bhpn", weighted_values, key_rows, precision=HIGHEST)
    keep_flags = (prior_segment == last_segment).astype(jnp.float32)
    start_state = jnp.zeros((head_count, head_size, state_size), jnp.float32)
    unused, incoming = lax.scan(carry_state, start_state, (local_states, span_total, keep_flags))
    reads = (bin_segment == prior_segment[:, None]).astype(jnp.float32)
    entry_decay = jnp.exp(cumulative) * reads[:, None, :]
    carried = jnp.einsum("btn,bhpn->bthp", query_rows, incoming, precision=HIGHEST)
    result = result + carried * jnp.transpose(entry_decay, (0, 2, 1))[:, :, :, None]
    result = result + d_skip[None, None, :, None] * head_values
    return result.reshape(row_count, head_count * head_size)


def pre_norm(residual, gain_row):
    scale_rows = lax.rsqrt(jnp.mean(residual * residual, axis=1, keepdims=True) + epsilon)
    return residual * scale_rows * gain_row[None, :]


def shard_squares(row_sums):
    return lax.psum(row_sums, "shard")


def shard_dots(row_sums):
    return lax.psum(row_sums, "shard")


def rows_product(left, right):
    return lax.dot_general(
        left, right, (((0,), (0,)), ((), ())), preferred_element_type=jnp.float32
    )


def back_product(left, right):
    return lax.dot_general(
        left, right, (((1,), (1,)), ((), ())), preferred_element_type=jnp.float32
    )


def branch_forward(normed, matrices, smalls, segment, square_total):
    proj_z = jnp.dot(normed, matrices[0], preferred_element_type=jnp.float32)
    proj_x = jnp.dot(normed, matrices[1], preferred_element_type=jnp.float32)
    proj_bc = jnp.dot(normed, matrices[2], preferred_element_type=jnp.float32)
    proj_dt = jnp.dot(normed, matrices[3], preferred_element_type=jnp.float32)
    core_fn = partial(mixer_core, segment=segment)
    core_out, core_back = jax.vjp(
        core_fn,
        proj_x,
        proj_bc,
        proj_dt,
        smalls[0],
        smalls[1],
        smalls[2],
        smalls[3],
        smalls[4],
        smalls[5],
        smalls[6],
    )
    gated_rows = core_out * jax.nn.silu(proj_z)
    inverse = lax.rsqrt(square_total(jnp.sum(gated_rows * gated_rows, axis=1)) / INNER + epsilon)
    mixed_rows = (gated_rows * inverse[:, None] * smalls[7][None, :]).astype(jnp.bfloat16)
    return (mixed_rows, (proj_z, core_out, core_back, gated_rows, inverse))


def branch_backward(d_mixed, kept_state, gain_row, dot_total):
    proj_z, core_out, core_back, gated_rows, inverse = kept_state
    grad_gate = jnp.sum(d_mixed * gated_rows * inverse[:, None], axis=0)
    d_hat = d_mixed * gain_row[None, :]
    dot_sum = dot_total(jnp.sum(d_hat * gated_rows, axis=1))
    d_gated = (
        inverse[:, None] * d_hat
        - gated_rows * (inverse * inverse * inverse * dot_sum / INNER)[:, None]
    )
    sigmoid_z = jax.nn.sigmoid(proj_z)
    d_core = d_gated * proj_z * sigmoid_z
    d_proj_z = d_gated * core_out * sigmoid_z * (1.0 + proj_z * (1.0 - sigmoid_z))
    core_grads = core_back(d_core)
    return (grad_gate, d_proj_z, core_grads)


def sum_replicas(parts):
    return (
        lax.psum(parts[0].astype(jnp.bfloat16), "rep").astype(jnp.float32),
        lax.psum(parts[1].astype(jnp.bfloat16), "rep").astype(jnp.float32),
        lax.psum(parts[2].astype(jnp.bfloat16), "rep").astype(jnp.float32),
        lax.psum(parts[3].astype(jnp.bfloat16), "rep").astype(jnp.float32),
        lax.psum(parts[4].astype(jnp.bfloat16), "rep").astype(jnp.float32),
        lax.psum(parts[5].astype(jnp.bfloat16), "rep").astype(jnp.float32),
        lax.psum(parts[6].astype(jnp.bfloat16), "rep").astype(jnp.float32),
        lax.psum(parts[7].astype(jnp.bfloat16), "rep").astype(jnp.float32),
        lax.psum(parts[8].astype(jnp.bfloat16), "rep").astype(jnp.float32),
        lax.psum(parts[9].astype(jnp.bfloat16), "rep").astype(jnp.float32),
        lax.psum(parts[10].astype(jnp.bfloat16), "rep").astype(jnp.float32),
        lax.psum(parts[11].astype(jnp.bfloat16), "rep").astype(jnp.float32),
        lax.psum(parts[12].astype(jnp.bfloat16), "rep").astype(jnp.float32),
        lax.psum(parts[13].astype(jnp.bfloat16), "rep").astype(jnp.float32),
    )


def on_device(
    hidden_in,
    cotangent,
    norm_gain,
    w_z,
    w_x,
    w_bc,
    w_dt,
    conv_x,
    conv_bc,
    bias_x,
    bias_bc,
    dt_bias,
    a_log,
    d_skip,
    gate_gain,
    w_out,
    seq_len,
    seq_owner,
    seq_start,
):
    shard_count = lax.axis_size("shard")
    shard_index = lax.axis_index("shard")
    first_device = lax.axis_index("rep") * shard_count
    own_rows = hidden_in.shape[0]
    own_segment, own_use = slot_segments(
        seq_len, seq_owner, seq_start, first_device + shard_index, own_rows
    )
    use_rows = own_use.astype(jnp.float32)[:, None]
    residual = hidden_in.astype(jnp.float32)
    d_residual = cotangent.astype(jnp.float32) * use_rows
    small_parts = (
        lax.all_gather(norm_gain.astype(jnp.bfloat16), "shard", axis=1, tiled=True).astype(
            norm_gain.dtype
        ),
        lax.all_gather(w_bc, "shard", axis=2, tiled=True),
        lax.all_gather(conv_bc.astype(jnp.bfloat16), "shard", axis=2, tiled=True).astype(
            conv_bc.dtype
        ),
        lax.all_gather(bias_bc.astype(jnp.bfloat16), "shard", axis=1, tiled=True).astype(
            bias_bc.dtype
        ),
    )
    member_ids = first_device + jnp.arange(shard_count, dtype=jnp.int32)
    group_segment = jax.vmap(
        lambda member: slot_segments(seq_len, seq_owner, seq_start, member, own_rows)[0]
    )(member_ids).reshape(-1)
    layer_index = 0
    normed_own = pre_norm(residual, small_parts[0][layer_index]).astype(jnp.bfloat16)
    normed = lax.all_gather(normed_own, "shard", axis=0, tiled=True)
    smalls = (
        conv_x[layer_index],
        small_parts[2][layer_index],
        bias_x[layer_index],
        small_parts[3][layer_index],
        dt_bias[layer_index],
        a_log[layer_index],
        d_skip[layer_index],
        gate_gain[layer_index],
    )
    matrices = (w_z[layer_index], w_x[layer_index], small_parts[1][layer_index], w_dt[layer_index])
    mixed_rows, kept_state = branch_forward(normed, matrices, smalls, group_segment, shard_squares)
    saved_layers = [(residual, normed, mixed_rows, kept_state)]

    def branch_term(row_start, row_count, mixed_rows=mixed_rows, out_weight=w_out[layer_index]):
        return jnp.dot(mixed_rows, out_weight, preferred_element_type=jnp.float32)

    residual = residual + lax.psum_scatter(
        branch_term(jnp.int32(0), lax.axis_size("shard") * own_rows).astype(jnp.bfloat16),
        "shard",
        scatter_dimension=0,
        tiled=True,
    ).astype(jnp.float32)
    layer_index = 0
    residual_in, normed, mixed_rows, kept_state = saved_layers[layer_index]
    out_cot = d_residual.astype(jnp.bfloat16)
    cot_all = lax.all_gather(out_cot, "shard", axis=0, tiled=True)
    grad_out = rows_product(mixed_rows, cot_all)
    d_mixed = back_product(cot_all, w_out[layer_index])
    grad_gate, d_proj_z, core_grads = branch_backward(
        d_mixed, kept_state, gate_gain[layer_index], shard_dots
    )
    bc_own = lax.psum_scatter(
        core_grads[1].astype(jnp.bfloat16), "shard", scatter_dimension=1, tiled=True
    )
    conv_own = lax.psum_scatter(
        core_grads[4].astype(jnp.bfloat16), "shard", scatter_dimension=1, tiled=True
    ).astype(jnp.float32)
    bias_own = lax.psum_scatter(
        core_grads[6].astype(jnp.bfloat16), "shard", scatter_dimension=0, tiled=True
    ).astype(jnp.float32)
    cot_z = d_proj_z.astype(jnp.bfloat16)
    cot_x = core_grads[0].astype(jnp.bfloat16)
    cot_dt = core_grads[2].astype(jnp.bfloat16)
    cotangents = (cot_z, cot_x, bc_own, cot_dt)
    matrices = (w_z[layer_index], w_x[layer_index], w_bc[layer_index], w_dt[layer_index])

    def input_term(row_start, row_count, cotangents=cotangents, matrices=matrices):
        running_sum = jnp.zeros((row_count, matrices[0].shape[0]), jnp.float32)
        for cot_part, matrix in zip(cotangents, matrices):
            running_sum = running_sum + back_product(cot_part, matrix)
        return running_sum

    d_normed = lax.psum_scatter(
        input_term(jnp.int32(0), lax.axis_size("shard") * own_rows).astype(jnp.bfloat16),
        "shard",
        scatter_dimension=0,
        tiled=True,
    ).astype(jnp.float32)
    norm_back = jax.vjp(pre_norm, residual_in, small_parts[0][layer_index])[1]
    d_previous, grad_norm_full = norm_back(d_normed)
    grad_norm = lax.psum_scatter(grad_norm_full, "shard", scatter_dimension=0, tiled=True)
    d_residual = d_residual + d_previous
    layer_grads = (
        grad_norm,
        rows_product(normed, cot_z),
        rows_product(normed, cot_x),
        rows_product(normed, bc_own),
        rows_product(normed, cot_dt),
        core_grads[3],
        conv_own,
        core_grads[5],
        bias_own,
        core_grads[7],
        core_grads[8],
        core_grads[9],
        grad_gate,
        grad_out,
    )
    collected = [layer_grads]
    ordered = collected[::-1]
    stacked = tuple(
        (jnp.stack([layer_grads[grad_slot] for layer_grads in ordered]) for grad_slot in range(14))
    )
    stacked = sum_replicas(stacked)
    hidden_out = residual * use_rows
    return (hidden_out, d_residual) + tuple(stacked)


def solution(mesh):
    in_specs = (
        P(("rep", "shard"), None),
        P(("rep", "shard"), None),
        P(None, "shard"),
        P(None, None, "shard"),
        P(None, None, "shard"),
        P(None, None, "shard"),
        P(None, None, "shard"),
        P(None, None, "shard"),
        P(None, None, "shard"),
        P(None, "shard"),
        P(None, "shard"),
        P(None, "shard"),
        P(None, "shard"),
        P(None, "shard"),
        P(None, "shard"),
        P(None, "shard", None),
        P(),
        P(),
        P(),
    )
    out_specs = (
        P(("rep", "shard"), None),
        P(("rep", "shard"), None),
        P(None, "shard"),
        P(None, None, "shard"),
        P(None, None, "shard"),
        P(None, None, "shard"),
        P(None, None, "shard"),
        P(None, None, "shard"),
        P(None, None, "shard"),
        P(None, "shard"),
        P(None, "shard"),
        P(None, "shard"),
        P(None, "shard"),
        P(None, "shard"),
        P(None, "shard"),
        P(None, "shard", None),
    )
    return jax.shard_map(
        on_device, mesh=mesh, in_specs=in_specs, out_specs=out_specs, check_vma=False
    )
```

profile of v0, /device:TPU:0, one launch (start us, length us, event | category | flops | bytes accessed | tf_op | source)
XLA Modules:
  0.0 437.6 jit_solution(8193885522419835834)
XLA Ops:
  15.0 5.2 %all_gather.18 = bf16[1,1024]{1,0:T(2,128)(2,1)S(1)} all-gather(bf16[1,512]{1,0:T(2,128)(2,1)S(1)} %convert_element_type.269), channel_id=1, replica_groups=mesh['rep'=16,'shard'=2] {'shard'}, dimensions={1}, use_global_device_ids=true | all-gather | bytes 3072 | tf_op jit(solution)/shard_map/all_gather | solution.py:211
  21.3 7.9 %all_gather.19 = bf16[256,1024]{1,0:T(8,128)(2,1)S(1)} all-gather(bf16[128,1024]{1,0:T(8,128)(2,1)S(1)} %fusion.84), channel_id=1, replica_groups=mesh['rep'=16,'shard'=2] {'shard'}, dimensions={0}, use_global_device_ids=true | all-gather | bytes 786432 | tf_op jit(solution)/shard_map/all_gather | solution.py:228
  32.2 2.3 fusion.19
  35.6 2.1 fusion.79
  37.7 2.8 reshape.543
  40.5 3.1 copy.204
  43.6 7.2 %all_gather.22 = bf16[1,1024,256]{2,1,0:T(8,128)(2,1)S(1)} all-gather(bf16[1,1024,128]{2,1,0:T(8,128)(2,1)S(1)} %copy-done.24), channel_id=1, replica_groups=mesh['rep'=16,'shard'=2] {'shard'}, dimensions={2}, use_global_device_ids=true | all-gather | bytes 786432 | tf_op jit(solution)/shard_map/all_gather | solution.py:214
  51.1 4.2 all_gather.21
  55.5 4.7 %all_gather.20 = bf16[1,256]{1,0:T(2,128)(2,1)S(1)} all-gather(bf16[1,128]{1,0:T(2,128)(2,1)S(1)} %convert_element_type.275), channel_id=1, replica_groups=mesh['rep'=16,'shard'=2] {'shard'}, dimensions={1}, use_global_device_ids=true | all-gather | bytes 768 | tf_op jit(solution)/shard_map/all_gather | solution.py:218
  62.5 4.9 %fusion.34 = f32[4,16,64,128]{3,2,1,0:T(8,128)} fusion(f32[4,64,128,1]{2,1,3,0:T(8,128)S(1)} %bitcast.247, f32[4,64,16,64]{1,3,2,0:T(8,128)} %copy.204, f32[4,64,16]{1,2,0:T(8,128)S(1)} %get-tuple-element.401), kind=kOutput, calls=%fused_computation.53 | convolution fusion | flops 402915328 | bytes 3293184 | tf_op jit(solution)/shard_map/jvp(bshp,bsn->bhpn)/dot_general | solution.py:82
  69.6 27.4 %while.36 = (s32[]{:T(128)}, f32[16,64,128]{2,1,0:T(8,128)S(1)}, f32[4,16,64,128]{3,2,1,0:T(8,128)}, f32[4,16]{1,0:T(4,128)}, f32[4,16,1,1]{1,3,2,0:T(1,128)}, /...) while((s32[]{:T(128)}, f32[16,64,128]{2,1,0:T(8,128)S(1)}, ...), condition=%wide.region_5.6_spmd.clone, body=%wide.region_4.5_spmd.clone.sunk | while | flops 524323 | bytes 2624072 | solution.py:85
  97.8 3.5 fusion.133
  102.7 5.3 %fusion.16 = f32[4,64,16,64]{1,3,2,0:T(8,128)} fusion(f32[4,64,16,64]{1,3,2,0:T(8,128)S(1)} %copy-done.4, f32[4,64,16,64]{1,3,2,0:T(8,128)S(1)} %fusion.133, f32[16]{0:T(128)S(1)} %bitcast.304, f32[4,64,16]{1,2,0:T(8,128)S(1)} %get-tuple-element.402, f32[4,16,64]{2,1,0:T(8,128)S(1)} %copy-done.39, f32[4,16,64]{2,1,0:T(8,128)S(1)} %bitcast.256, ...), kind=kOutput, calls=%fused_computation.28 | convolution fusion | flops 203685888 | bytes 3276864 | tf_op jit(solution)/shard_map/jvp(bhts,bshp->bthp)/dot_general | solution.py:75
  108.0 3.1 copy.210
  111.1 2.7 reshape.548
  113.9 3.4 multiply_reduce_fusion.11
  117.3 5.0 %psum.112 = f32[256]{0:T(256)S(1)} all-reduce(f32[256]{0:T(256)S(1)} %get-tuple-element.378), channel_id=1, replica_groups=mesh['rep'=16,'shard'=2] {'shard'}, use_global_device_ids=true, to_apply=%region_7.8 | all-reduce | flops 256 | bytes 2048 | tf_op jit(solution)/shard_map/psum | solution.py:100
  123.0 7.0 %all_gather.23 = bf16[256,1024]{1,0:T(8,128)(2,1)S(1)} all-gather(bf16[128,1024]{1,0:T(8,128)(2,1)S(1)} %fusion.92), channel_id=1, replica_groups=mesh['rep'=16,'shard'=2] {'shard'}, dimensions={0}, use_global_device_ids=true | all-gather | bytes 786432 | tf_op jit(solution)/shard_map/all_gather | solution.py:255
  130.0 4.5 %multiply_reduce_fusion.4 = (bf16[1024]{0:T(1024)(128)(2,1)}, f32[256]{0:T(256)S(1)}, f32[256,1024]{1,0:T(8,128)}) fusion(f32[256,1024]{1,0:T(8,128)} %get-tuple-element.379, f32[256]{0:T(256)S(1)} %add_rsqrt_fusion, f32[1024]{0:T(1024)S(1)} %bitcast.265, bf16[256,1024]{1,0:T(8,128)(2,1)S(1)} %all_gather.23, bf16[1,1024,1024]{2,1,0:T(8,128)(2,1)} %param.38), kind=kOutput, calls=%fused_computation.84 | convolution fusion | flops 538442496 | bytes 4726784 | tf_op jit(solution)/shard_map/dot_general | solution.py:114
  134.6 5.1 %psum.113 = f32[256]{0:T(256)S(1)} all-reduce(f32[256]{0:T(256)S(1)} %get-tuple-element.307), channel_id=1, replica_groups=mesh['rep'=16,'shard'=2] {'shard'}, use_global_device_ids=true, to_apply=%region_11.12 | all-reduce | flops 256 | bytes 2048 | tf_op jit(solution)/shard_map/psum | solution.py:104
  139.7 5.2 %multiply_reduce_fusion.5 = (f32[1024]{0:T(1024)}, f32[256,1024]{1,0:T(8,128)}, bf16[256,1024]{1,0:T(8,128)(2,1)}) fusion(f32[256,1024]{1,0:T(8,128)} %get-tuple-element.383, f32[256,1024]{1,0:T(8,128)} %get-tuple-element.419, f32[256,1024]{1,0:T(8,128)} %get-tuple-element.379, f32[256]{0:T(256)S(1)} %fusion.119, f32[256,1024]{1,0:T(8,128)} %get-tuple-element.420, ...), kind=kLoop, calls=%fused_computation.85 | loop fusion | flops 5766144 | bytes 6825984 | tf_op jit(solution)/shard_map/transpose(jvp())/reduce_sum | solution.py:90
  144.8 2.8 reshape.549
  147.7 3.1 copy.211
  150.8 7.4 %fusion.58 = (f32[4,16,64]{2,1,0:T(8,128)}, f32[4,16,64]{2,1,0:T(8,128)}, f32[4,16,64]{2,1,0:T(8,128)}, f32[4,64,64]{2,1,0:T(8,128)}) fusion(f32[4,16,64]{2,1,0:T(8,128)S(1)} %copy-done.40, f32[4,16,64]{2,1,0:T(8,128)S(1)} %bitcast.257, f32[4,64,64]{2,1,0:T(8,128)S(1)} %copy-done.30, pred[4,64,64]{2,1,0:T(8,128)(4,1)S(1)} %copy-done.37, ...), kind=kOutput, calls=%fused_computation.71 | convolution fusion | flops 205230080 | bytes 2326528 | tf_op jit(solution)/shard_map/transpose(jvp(bhts,bshp->bthp))/dot_general | solution.py:75
  158.1 4.2 fusion.49
  162.4 3.3 fusion.30
  167.3 22.3 %while.37 = (s32[]{:T(128)}, f32[16,64,128]{2,1,0:T(8,128)S(1)}, f32[4,16,64,128]{3,2,1,0:T(8,128)}, f32[4,16]{1,0:T(4,128)S(1)}, f32[4,16,64,128]{3,2,1,0:T(8,1...) while((s32[]{:T(128)}, f32[16,64,128]{2,1,0:T(8,128)S(1)}, ...), condition=%wide.region_14.15_spmd.clone, body=%wide.region_12.14_spmd.clone.sunk | while | flops 786452 | bytes 3146480 | solution.py:85
  190.2 5.9 %fusion.46 = f32[4,64,128]{2,1,0:T(8,128)S(1)} fusion(f32[4,16,64,128]{3,2,1,0:T(8,128)} %get-tuple-element.243, f32[4,64,16,64]{1,3,2,0:T(8,128)} %copy.204, f32[4,64,16]{1,2,0:T(8,128)S(1)} %get-tuple-element.401), kind=kOutput, calls=%fused_computation.63 | convolution fusion | flops 402915328 | bytes 3293184 | tf_op jit(solution)/shard_map/transpose(jvp(bshp,bsn->bhpn))/dot_general | solution.py:82
  199.6 4.3 multiply_reduce_fusion.2
  205.6 5.7 %bitcast_add_fusion.2 = f32[4,64,16,64]{1,3,2,0:T(8,128)} fusion(f32[4,64,16,64]{1,3,2,0:T(8,128)S(1)} %get-tuple-element.422, f32[4,64,16,64]{1,3,2,0:T(8,128)S(1)} %copy-done.2, f32[4,16,64,64]{2,1,3,0:T(8,128)S(1)} %bitcast.246, f32[16]{0:T(128)S(1)} %bitcast.305, f32[4,64,16]{1,2,0:T(8,128)S(1)} %get-tuple-element.401, f32[4,16,64]{2,1,0:T(8,128)S(1)} %copy-done.41, ...), kind=kOutput, calls=%fused_computation.14 | convolution fusion | flops 203685888 | bytes 4325440 | tf_op jit(solution)/shard_map/transpose(jvp(bhts,bshp->bthp))/dot_general | solution.py:75
  211.3 3.1 copy.215
  214.3 2.7 reshape.550
  217.1 5.0 %multiply_reduce_fusion.9 = (f32[1024]{0:T(1024)S(1)}, f32[1024]{0:T(1024)}, f32[1024]{0:T(1024)}, f32[1024]{0:T(1024)}, bf16[1024]{0:T(1024)(128)(2,1)}, /*index=5*/f32[256,1024]{1,0:T(8,128)S(1)}) fusion(f32[256,1024]{1,0:T(8,128)} %copy-done.7, f32[256]{0:T(256)S(1)} %copy-done.52, f32[256]{0:T(256)S(1)} %copy-done.50, f32[256]{0:T(256)S(1)} %copy-done.48, ...), kind=kLoop, calls=%fused_computation.89 | loop fusion | flops 5499904 | bytes 4215808 | tf_op jit(solution)/shard_map/transpose(jvp())/reduce_sum | solution.py:36
  222.2 1.9 multiply_multiply_fusion.2
  224.6 1.8 reduce_window_sum.23
  230.2 1.9 fusion.62
  236.9 3.5 fusion.42
  240.4 3.1 convert_bitcast_fusion.1
  243.6 2.1 convert_bitcast_fusion.2
  245.6 2.1 convert_bitcast_fusion
  251.6 5.2 %all-reduce.27 = bf16[256]{0:T(256)(128)(2,1)S(1)} all-reduce(bf16[256]{0:T(256)(128)(2,1)S(1)} %copy-done.99), channel_id=7, replica_groups=mesh['rep'=16,'shard'=2] {'shard'}, use_global_device_ids=true, to_apply=%region_47.48.clone | all-reduce | flops 256 | bytes 1024
  259.2 5.0 %all-reduce.26 = bf16[1024]{0:T(1024)(128)(2,1)S(1)} all-reduce(f32[1024]{0:T(1024)S(1)} %get-tuple-element.317), channel_id=5, replica_groups=mesh['rep'=16,'shard'=2] {'shard'}, use_global_device_ids=true, to_apply=%region_27.28.clone | all-reduce | flops 1024 | bytes 6144
  264.3 60.8 %all-reduce.28 = (bf16[1,512]{1,0:T(2,128)(2,1)S(1)}, bf16[1,1024,16]{1,2,0:T(8,128)(2,1)S(1)}, bf16[1,4,1024]{2,1,0:T(4,128)(2,1)S(1)}, bf16[1,4,128]{2,1,0:T(4...) all-reduce(bf16[1,512]{1,0:T(2,128)(2,1)S(1)} %convert_element_type, ...), channel_id=1, replica_groups=mesh['rep'=16,'shard'=2] {'rep'}, use_global_device_ids=true, to_apply=%region_28.29 | all-reduce | flops 23728 | bytes 94912 | tf_op jit(solution)/shard_map/psum | solution.py:162
  330.8 2.4 fusion.86
  333.2 87.4 %all-reduce.32.cloned.1.call-done = (bf16[1,1024,1024]{2,1,0:T(8,128)(2,1)}, bf16[1,1024,1024]{2,1,0:T(8,128)(2,1)}, bf16[1,1024,128]{2,1,0:T(8,128)(2,1)}, bf16[1,1024,1024]{2,1,0:T(8,128)(2,1)}) async-done(((bf16[1,1024,1024]{2,1,0:T(8,128)(2,1)}, bf16[1,1024,1024]{2,1,0:T(8,128)(2,1)}, bf16[1,1024,128]{2,1,0:T(8,128)(2,1)}, bf16[1,1024,1024]{2,1,0:T(8,128)(2,1)}), (bf16[1,1024,1024]{2,1,0:T(8,128)(2,1)}, ...) | async-done | bytes 6553616 | tf_op jit(solution)/shard_map/psum | solution.py:163
  420.6 4.2 convert_element_type.299
  424.8 2.5 convert_element_type.302
  427.3 2.5 convert_element_type.334
  (373 shorter events, 97.4 us)
Async XLA Ops:
  7.2 106.6 %copy-start = (bf16[1,1024,1024]{2,1,0:T(8,128)(2,1)S(1)}, bf16[1,1024,1024]{2,1,0:T(8,128)(2,1)}, u32[]{:S(2)}) copy-start(bf16[1,1024,1024]{2,1,0:T(8,128)(2,1)} %param.26) | copy-start | bytes 6291460
  7.2 226.9 %reduce-scatter.13.cloned.1.call-start = ((), (), s32[]{:S(2)}) async-start(), calls=%async_computation.6 | async-start | bytes 196608
  8.1 12.1 %copy-start.70 = (s32[256]{0:T(256)}, s32[256]{0:T(256)S(1)}, u32[]{:S(2)}) copy-start(s32[256]{0:T(256)S(1)} %add.321) | copy-start | bytes 3076
  12.6 48.6 %copy-start.45 = (f32[4,64]{1,0:T(4,128)}, f32[4,64]{1,0:T(4,128)S(1)}, u32[]{:S(2)}) copy-start(f32[4,64]{1,0:T(4,128)S(1)} %get-tuple-element.410) | copy-start | bytes 3076
  14.3 5.9 %copy-start.86 = (f32[128]{0:T(128)}, f32[128]{0:T(128)S(1)}, u32[]{:S(2)}) copy-start(f32[128]{0:T(128)S(1)} %fusion.121) | copy-start | bytes 1540
  32.2 28.0 %copy-start.47 = (f32[256]{0:T(256)}, f32[256]{0:T(256)S(1)}, u32[]{:S(2)}) copy-start(f32[256]{0:T(256)S(1)} %get-tuple-element.415) | copy-start | bytes 3076
  32.2 28.0 %copy-start.49 = (f32[256]{0:T(256)}, f32[256]{0:T(256)S(1)}, u32[]{:S(2)}) copy-start(f32[256]{0:T(256)S(1)} %get-tuple-element.416) | copy-start | bytes 3076
  32.2 28.0 %copy-start.51 = (f32[256]{0:T(256)}, f32[256]{0:T(256)S(1)}, u32[]{:S(2)}) copy-start(f32[256]{0:T(256)S(1)} %get-tuple-element.417) | copy-start | bytes 3076
  34.5 6.0 %copy-start.53 = (f32[1,1,1024]{2,1,0:T(1,128)}, f32[1,1,1024]{2,1,0:T(1,128)S(1)}, u32[]{:S(2)}) copy-start(f32[1,1,1024]{2,1,0:T(1,128)S(1)} %get-tuple-element.406) | copy-start | bytes 12292
  34.5 6.0 %copy-start.55 = (f32[1,1,1024]{2,1,0:T(1,128)}, f32[1,1,1024]{2,1,0:T(1,128)S(1)}, u32[]{:S(2)}) copy-start(f32[1,1,1024]{2,1,0:T(1,128)S(1)} %get-tuple-element.407) | copy-start | bytes 12292
  34.5 6.0 %copy-start.57 = (f32[1,1,1024]{2,1,0:T(1,128)}, f32[1,1,1024]{2,1,0:T(1,128)S(1)}, u32[]{:S(2)}) copy-start(f32[1,1,1024]{2,1,0:T(1,128)S(1)} %get-tuple-element.408) | copy-start | bytes 12292
  34.6 5.9 %copy-start.59 = (f32[1,1,1024]{2,1,0:T(1,128)}, f32[1,1,1024]{2,1,0:T(1,128)S(1)}, u32[]{:S(2)}) copy-start(f32[1,1,1024]{2,1,0:T(1,128)S(1)} %get-tuple-element.405) | copy-start | bytes 12292
  43.6 7.5 %copy-start.94 = (f32[1,4,128]{2,1,0:T(4,128)S(1)}, f32[1,4,128]{2,1,0:T(4,128)}, u32[]{:S(2)}) copy-start(f32[1,4,128]{2,1,0:T(4,128)} %param.31) | copy-start | bytes 6148
  43.6 11.8 %copy-start.100 = (f32[1,128]{1,0:T(1,128)S(1)}, f32[1,128]{1,0:T(1,128)}, u32[]{:S(2)}) copy-start(f32[1,128]{1,0:T(1,128)} %param.33) | copy-start | bytes 1540
  51.1 10.0 %copy-start.20 = (f32[256,256]{1,0:T(8,128)}, f32[256,256]{1,0:T(8,128)S(1)}, u32[]{:S(2)}) copy-start(f32[256,256]{1,0:T(8,128)S(1)} %fusion.90) | copy-start | bytes 786436
  55.4 5.7 %copy-start.74 = (f32[1,1,256]{2,1,0:T(1,128)}, f32[1,1,256]{2,1,0:T(1,128)S(1)}, u32[]{:S(2)}) copy-start(f32[1,1,256]{2,1,0:T(1,128)S(1)} %get-tuple-element.411) | copy-start | bytes 3076
  55.4 5.7 %copy-start.76 = (f32[1,1,256]{2,1,0:T(1,128)}, f32[1,1,256]{2,1,0:T(1,128)S(1)}, u32[]{:S(2)}) copy-start(f32[1,1,256]{2,1,0:T(1,128)S(1)} %get-tuple-element.412) | copy-start | bytes 3076
  55.4 5.7 %copy-start.78 = (f32[1,1,256]{2,1,0:T(1,128)}, f32[1,1,256]{2,1,0:T(1,128)S(1)}, u32[]{:S(2)}) copy-start(f32[1,1,256]{2,1,0:T(1,128)S(1)} %get-tuple-element.413) | copy-start | bytes 3076
  113.8 8.5 %copy-start.89 = (s32[256]{0:T(256)S(1)}, s32[256]{0:T(256)}, u32[]{:S(2)}) copy-start(s32[256]{0:T(256)} %param.40) | copy-start | bytes 3076
  113.8 8.5 %copy-start.69 = (s32[256]{0:T(256)S(1)}, s32[256]{0:T(256)}, u32[]{:S(2)}) copy-start(s32[256]{0:T(256)} %param.41) | copy-start | bytes 3076
  113.8 8.5 %copy-start.71 = (s32[256]{0:T(256)S(1)}, s32[256]{0:T(256)}, u32[]{:S(2)}) copy-start(s32[256]{0:T(256)} %copy-done.70) | copy-start | bytes 3076
  113.8 9.0 %copy-start.27 = (bf16[128,1024]{1,0:T(8,128)(2,1)S(1)}, bf16[128,1024]{1,0:T(8,128)(2,1)}, u32[]{:S(2)}) copy-start(bf16[128,1024]{1,0:T(8,128)(2,1)} %param.24) | copy-start | bytes 786436
  113.9 16.2 %copy-start.43 = (f32[1,1024]{1,0:T(1,128)S(1)}, f32[1,1024]{1,0:T(1,128)}, u32[]{:S(2)}) copy-start(f32[1,1024]{1,0:T(1,128)} %param.37) | copy-start | bytes 12292
  122.8 7.2 %copy-start.90 = (f32[128]{0:T(128)}, f32[128]{0:T(128)S(1)}, u32[]{:S(2)}) copy-start(f32[128]{0:T(128)S(1)} %convert_element_type.285) | copy-start | bytes 1540
  130.0 9.6 %copy-start.73 = (f32[256]{0:T(256)S(1)}, f32[256]{0:T(256)}, u32[]{:S(2)}) copy-start(f32[256]{0:T(256)} %copy-done.72) | copy-start | bytes 3076
  150.7 7.4 %copy-start.1 = (f32[4,64,16,64]{1,3,2,0:T(8,128)S(1)}, f32[4,64,16,64]{1,3,2,0:T(8,128)}, u32[]{:S(2)}) copy-start(f32[4,64,16,64]{1,3,2,0:T(8,128)} %copy.211) | copy-start | bytes 3145732
  150.7 7.4 %copy-start.3 = (f32[4,16,64,128]{3,2,1,0:T(8,128)S(1)}, f32[4,16,64,128]{3,2,1,0:T(8,128)}, u32[]{:S(2)}) copy-start(f32[4,16,64,128]{3,2,1,0:T(8,128)} %get-tuple-element.579) | copy-start | bytes 6291460
  190.1 6.0 %copy-start.32 = (f32[4,64,128]{2,1,0:T(8,128)S(1)}, f32[4,64,128]{2,1,0:T(8,128)}, u32[]{:S(2)}) copy-start(f32[4,64,128]{2,1,0:T(8,128)} %fusion.49) | copy-start | bytes 393220
  190.1 6.0 %copy-start.33 = (f32[4,64,64]{2,1,0:T(8,128)S(1)}, f32[4,64,64]{2,1,0:T(8,128)}, u32[]{:S(2)}) copy-start(f32[4,64,64]{2,1,0:T(8,128)} %get-tuple-element.305) | copy-start | bytes 196612
  190.1 6.6 %copy-start.21 = (f32[256,256]{1,0:T(8,128)S(1)}, f32[256,256]{1,0:T(8,128)}, u32[]{:S(2)}) copy-start(f32[256,256]{1,0:T(8,128)} %copy-done.20) | copy-start | bytes 786436
  190.1 6.7 %copy-start.26 = (f32[256,256]{1,0:T(8,128)S(1)}, f32[256,256]{1,0:T(8,128)}, u32[]{:S(2)}) copy-start(f32[256,256]{1,0:T(8,128)} %get-tuple-element.381) | copy-start | bytes 786436
  190.1 6.7 %copy-start.48 = (f32[256]{0:T(256)S(1)}, f32[256]{0:T(256)}, u32[]{:S(2)}) copy-start(f32[256]{0:T(256)} %copy-done.47) | copy-start | bytes 3076
  190.2 6.7 %copy-start.50 = (f32[256]{0:T(256)S(1)}, f32[256]{0:T(256)}, u32[]{:S(2)}) copy-start(f32[256]{0:T(256)} %copy-done.49) | copy-start | bytes 3076
  190.2 6.7 %copy-start.52 = (f32[256]{0:T(256)S(1)}, f32[256]{0:T(256)}, u32[]{:S(2)}) copy-start(f32[256]{0:T(256)} %copy-done.51) | copy-start | bytes 3076
  198.7 58.5 %reduce-scatter.15.cloned.1.call-start = ((), (), s32[]{:S(2)}) async-start(), calls=%async_computation.7 | async-start | bytes 98304
  199.6 58.4 %reduce-scatter.11.cloned.1.call-start = ((), (), s32[]{:S(2)}) async-start(), calls=%async_computation.5 | async-start | bytes 786432 | tf_op jit(solution)/shard_map/reduce_scatter | solution.py:282
  222.2 6.2 %copy-start.15 = (bf16[256,1024]{1,0:T(8,128)(2,1)S(1)}, bf16[256,1024]{1,0:T(8,128)(2,1)}, u32[]{:S(2)}) copy-start(bf16[256,1024]{1,0:T(8,128)(2,1)} %get-tuple-element.388) | copy-start | bytes 1572868
  236.8 93.9 %reduce-scatter.9.cloned.1.call-start = ((), (), s32[]{:S(2)}) async-start(), calls=%async_computation.4 | async-start | bytes 786432 | tf_op jit(solution)/shard_map/reduce_scatter | solution.py:246
  240.4 180.2 %all-reduce.32.cloned.1.call-start = ((), (), s32[]{:S(2)}) async-start(), calls=%async_computation.8 | async-start | bytes 13107200 | tf_op jit(solution)/shard_map/psum | solution.py:163
  248.8 8.1 %copy-start.66 = (f32[1024]{0:T(1024)S(1)}, f32[1024]{0:T(1024)}, u32[]{:S(2)}) copy-start(f32[1024]{0:T(1024)} %get-tuple-element.309) | copy-start | bytes 12292
  248.9 8.1 %copy-start.67 = (f32[1024]{0:T(1024)S(1)}, f32[1024]{0:T(1024)}, u32[]{:S(2)}) copy-start(f32[1024]{0:T(1024)} %get-tuple-element.310) | copy-start | bytes 12292
  248.9 8.0 %copy-start.68 = (f32[1024]{0:T(1024)S(1)}, f32[1024]{0:T(1024)}, u32[]{:S(2)}) copy-start(f32[1024]{0:T(1024)} %get-tuple-element.311) | copy-start | bytes 12292
  248.9 8.2 %copy-start.101 = (f32[1,16]{1,0:T(1,128)S(1)}, f32[1,16]{1,0:T(1,128)}, u32[]{:S(2)}) copy-start(f32[1,16]{1,0:T(1,128)} %param.35) | copy-start | bytes 196
  248.9 9.1 %copy-start.17 = (bf16[128,1024]{1,0:T(8,128)(2,1)S(1)}, bf16[128,1024]{1,0:T(8,128)(2,1)}, u32[]{:S(2)}) copy-start(bf16[128,1024]{1,0:T(8,128)(2,1)} %param.23) | copy-start | bytes 786436
  248.9 9.1 %copy-start.87 = (f32[128]{0:T(128)S(1)}, f32[128]{0:T(128)}, u32[]{:S(2)}) copy-start(f32[128]{0:T(128)} %copy-done.86) | copy-start | bytes 1540
  248.9 81.8 %copy-start.98 = (f32[128]{0:T(128)S(1)}, f32[128]{0:T(128)}, u32[]{:S(2)}) copy-start(f32[128]{0:T(128)} %copy-done.97) | copy-start | bytes 1540
  248.9 81.9 %copy-start.28 = (bf16[128,1024]{1,0:T(8,128)(2,1)S(1)}, bf16[128,1024]{1,0:T(8,128)(2,1)}, u32[]{:S(2)}) copy-start(bf16[128,1024]{1,0:T(8,128)(2,1)} %param.24) | copy-start | bytes 786436
  248.9 81.8 %copy-start.91 = (f32[128]{0:T(128)S(1)}, f32[128]{0:T(128)}, u32[]{:S(2)}) copy-start(f32[128]{0:T(128)} %copy-done.90) | copy-start | bytes 1540
  (60 other events, 151.4 us)
Sparse Core Ops, SparseCore 0:
  198.8 11.6 reduce-scatter.12
  213.3 9.8 reduce-scatter.14
  237.0 16.0 reduce-scatter.10
  255.8 14.5 reduce-scatter.8
  275.5 145.0 all-reduce.31
where the time goes:
time: 443 us; the launch traced here: 438 us
  blocking collectives  117 us (26%)
  waiting for transfers between devices  87.5 us (20%)
  other arithmetic  83 us (19%)
  matrix products  74.8 us (17%)
  local copies, waits for them, and re-layouts  57.6 us (13%)
  between operations  16.8 us (4%)
    psum x1, waiting for transfers between devices, sum_replicas(): lax.psum(parts[1].astype(jnp.bfloat16), 'rep').astype(jnp.float32)  87.4 us
    psum x1, blocking collectives, sum_replicas(): lax.psum(parts[0].astype(jnp.bfloat16), 'rep').astype(jnp.float32)  60.8 us
    dot_general x3, matrix products, mixer_core(): jnp.einsum('bhts,bshp->bthp', mixing, head_values, precision=HIGHEST)  18.3 us
    dot_general x3, matrix products, mixer_core(): jnp.einsum('bshp,bsn->bhpn', weighted_values, key_rows, precision=HIGHEST)  15.1 us
    dynamic_update_slice x12, other arithmetic, mixer_core(): lax.scan(carry_state, start_state, (local_states, span_total, keep_flags))  11.4 us
    dot_general x3, matrix products, mixer_core(): jnp.einsum('btn,bhpn->bthp', query_rows, incoming, precision=HIGHEST)  11.1 us
    unnamed x2, blocking collectives  10.2 us
    dynamic_slice x8, local copies, waits for them, and re-layouts, mixer_core(): lax.scan(carry_state, start_state, (local_states, span_total, keep_flags))  9.92 us
  transfers between devices with their start and end apart: 5, of which 1 were waited for; matrix products, arithmetic and copies ran while one was open for 13% of the time, Pallas kernels for 0%

commit v1 on v0

--- a/solution.py
+++ b/solution.py
@@ -8,6 +8,11 @@
 INNER = 2048
 epsilon = 1e-05
 HIGHEST = lax.Precision.HIGHEST
+
+
+def gather_and_add(x, axis):
+    terms = lax.all_gather(x, axis)
+    return jnp.sum(terms, axis=0)
 
 
 def slot_segments(seq_len, seq_owner, seq_start, device, row_count):
@@ -160,7 +165,7 @@
 def sum_replicas(parts):
     return (
         lax.psum(parts[0].astype(jnp.bfloat16), "rep").astype(jnp.float32),
-        lax.psum(parts[1].astype(jnp.bfloat16), "rep").astype(jnp.float32),
+        gather_and_add(parts[1].astype(jnp.bfloat16), "rep").astype(jnp.float32),
         lax.psum(parts[2].astype(jnp.bfloat16), "rep").astype(jnp.float32),
         lax.psum(parts[3].astype(jnp.bfloat16), "rep").astype(jnp.float32),
         lax.psum(parts[4].astype(jnp.bfloat16), "rep").astype(jnp.float32),

time: 443 us -> 584 us (1.32)
  waiting for transfers between devices: 87.5 us -> 222 us
  other arithmetic: 83 us -> 97 us
  local copies, waits for them, and re-layouts: 57.6 us -> 51.4 us
    all_gather x0 -> x1, waiting for transfers between devices: none -> 162 us  [gather_and_add(): terms = lax.all_gather(x, axis)]
    psum x1, waiting for transfers between devices: 87.4 us -> 59.4 us  [sum_replicas(): lax.psum(parts[2].astype(jnp.bfloat16), 'rep').astype(jnp.float32)]
    reduce_sum x0 -> x1, other arithmetic: none -> 13.2 us  [gather_and_add(): return jnp.sum(terms, axis=0)]
  transfers between devices with their start and end apart: 5 -> 6, of which waited for: 1 -> 2; matrix products, arithmetic and copies ran while one was open for 13% -> 10% of each run, Pallas kernels for 0% -> 0%
where the time goes in v1:
time: 584 us; the launch traced here: 578 us
  waiting for transfers between devices  222 us (38%)
  blocking collectives  117 us (20%)
  other arithmetic  97 us (17%)
  matrix products  73.3 us (13%)
  local copies, waits for them, and re-layouts  51.4 us (9%)
  between operations  16.9 us (3%)
    all_gather x1, waiting for transfers between devices, gather_and_add(): terms = lax.all_gather(x, axis)  162 us
    psum x1, blocking collectives, sum_replicas(): lax.psum(parts[0].astype(jnp.bfloat16), 'rep').astype(jnp.float32)  60 us
    psum x1, waiting for transfers between devices, sum_replicas(): lax.psum(parts[2].astype(jnp.bfloat16), 'rep').astype(jnp.float32)  59.4 us
    dot_general x3, matrix products, mixer_core(): jnp.einsum('bhts,bshp->bthp', mixing, head_values, precision=HIGHEST)  16.8 us
    dot_general x3, matrix products, mixer_core(): jnp.einsum('bshp,bsn->bhpn', weighted_values, key_rows, precision=HIGHEST)  15.1 us
    reduce_sum x1, other arithmetic, gather_and_add(): return jnp.sum(terms, axis=0)  13.2 us
  transfers between devices with their start and end apart: 6, of which 2 were waited for; matrix products, arithmetic and copies ran while one was open for 10% of the time, Pallas kernels for 0%

profile of v1, /device:TPU:0, one launch (start us, length us, event | category | flops | bytes accessed | tf_op | source)
XLA Modules:
  0.0 578.3 jit_solution(8911318788968390335)
XLA Ops:
  12.1 5.2 all_gather.24
  19.6 7.9 %all_gather.25 = bf16[256,1024]{1,0:T(8,128)(2,1)S(1)} all-gather(bf16[128,1024]{1,0:T(8,128)(2,1)S(1)} %fusion.84), channel_id=1, replica_groups=mesh['rep'=16,'shard'=2] {'shard'}, dimensions={0}, use_global_device_ids=true | all-gather | bytes 786432 | tf_op jit(solution)/shard_map/all_gather | solution.py:233
  28.4 2.3 fusion.19
  31.7 2.1 fusion.79
  33.8 2.8 reshape.555
  36.7 3.1 copy.204
  39.8 7.2 %all_gather.28 = bf16[1,1024,256]{2,1,0:T(8,128)(2,1)S(1)} all-gather(bf16[1,1024,128]{2,1,0:T(8,128)(2,1)S(1)} %copy-done.29), channel_id=1, replica_groups=mesh['rep'=16,'shard'=2] {'shard'}, dimensions={2}, use_global_device_ids=true | all-gather | bytes 786432 | tf_op jit(solution)/shard_map/all_gather | solution.py:219
  48.4 4.2 all_gather.27
  52.7 4.4 all_gather.26
  65.1 4.9 fusion.34
  72.1 22.8 %while.36 = (s32[]{:T(128)}, f32[16,64,128]{2,1,0:T(8,128)S(1)}, f32[4,16,64,128]{3,2,1,0:T(8,128)}, f32[4,16]{1,0:T(4,128)}, f32[4,16,1,1]{1,3,2,0:T(1,128)}, /...) while((s32[]{:T(128)}, f32[16,64,128]{2,1,0:T(8,128)S(1)}, ...), condition=%wide.region_5.6_spmd.clone, body=%wide.region_4.5_spmd.clone.sunk | while | flops 524323 | bytes 2623064 | solution.py:90
  95.7 3.5 fusion.133
  100.6 5.3 fusion.16
  105.9 3.1 copy.210
  109.0 2.8 reshape.560
  111.8 3.4 multiply_reduce_fusion.11
  115.2 5.5 psum.105
  124.0 7.0 %all_gather.29 = bf16[256,1024]{1,0:T(8,128)(2,1)S(1)} all-gather(bf16[128,1024]{1,0:T(8,128)(2,1)S(1)} %fusion.92), channel_id=1, replica_groups=mesh['rep'=16,'shard'=2] {'shard'}, dimensions={0}, use_global_device_ids=true | all-gather | bytes 786432 | tf_op jit(solution)/shard_map/all_gather | solution.py:260
  131.1 4.5 multiply_reduce_fusion.4
  135.6 6.0 %psum.106 = f32[256]{0:T(256)} all-reduce(f32[256]{0:T(256)} %get-tuple-element.307), channel_id=1, replica_groups=mesh['rep'=16,'shard'=2] {'shard'}, use_global_device_ids=true, to_apply=%region_11.12 | all-reduce | flops 256 | bytes 2048 | tf_op jit(solution)/shard_map/psum | solution.py:109
  142.3 5.2 multiply_reduce_fusion.5
  147.4 2.8 reshape.561
  150.2 3.1 copy.211
  153.3 7.3 %fusion.58 = (f32[4,16,64]{2,1,0:T(8,128)}, f32[4,16,64]{2,1,0:T(8,128)}, f32[4,16,64]{2,1,0:T(8,128)}, f32[4,64,64]{2,1,0:T(8,128)}) fusion(f32[4,16,64]{2,1,0:T(8,128)} %get-tuple-element.399, f32[4,16,64]{2,1,0:T(8,128)S(1)} %bitcast.260, f32[4,64,64]{2,1,0:T(8,128)} %copy-done.33, pred[4,64,64]{2,1,0:T(8,128)(4,1)S(1)} %compare_and_fusion, ...), kind=kOutput, calls=%fused_computation.72 | convolution fusion | flops 205230080 | bytes 2326528 | tf_op jit(solution)/shard_map/transpose(jvp(bhts,bshp->bthp))/dot_general | solution.py:80
  160.6 3.3 fusion.30
  164.0 4.3 fusion.49
  169.8 19.6 %while.37 = (s32[]{:T(128)}, f32[16,64,128]{2,1,0:T(8,128)S(1)}, f32[4,16,64,128]{3,2,1,0:T(8,128)}, f32[4,16]{1,0:T(4,128)S(1)}, f32[4,16,64,128]{3,2,1,0:T(8,1...) while((s32[]{:T(128)}, f32[16,64,128]{2,1,0:T(8,128)S(1)}, ...), condition=%wide.region_14.15_spmd.clone, body=%wide.region_12.14_spmd.clone.sunk | while | flops 786452 | bytes 3146488 | solution.py:90
  190.1 5.9 %fusion.46 = f32[4,64,128]{2,1,0:T(8,128)S(1)} fusion(f32[4,16,64,128]{3,2,1,0:T(8,128)} %get-tuple-element.243, f32[4,64,16,64]{1,3,2,0:T(8,128)} %copy.204, f32[4,64,16]{1,2,0:T(8,128)S(1)} %get-tuple-element.400), kind=kOutput, calls=%fused_computation.64 | convolution fusion | flops 402915328 | bytes 3293184 | tf_op jit(solution)/shard_map/transpose(jvp(bshp,bsn->bhpn))/dot_general | solution.py:87
  199.5 4.3 multiply_reduce_fusion.2
  206.7 4.2 bitcast_add_fusion.2
  210.8 2.2 copy.215
  213.0 2.9 reshape.562
  216.0 2.4 multiply_reduce_fusion.9
  222.4 2.8 fusion.62
  230.4 3.2 fusion.42
  233.7 2.1 convert_bitcast_fusion.1
  235.7 2.2 convert_bitcast_fusion
  240.0 2.1 convolution_convert_fusion
  244.3 4.9 all-reduce.27
  251.6 4.9 all-reduce.26
  256.6 60.0 %all-reduce.28 = (bf16[1,512]{1,0:T(2,128)(2,1)S(1)}, bf16[1,1024,16]{1,2,0:T(8,128)(2,1)S(1)}, bf16[1,4,1024]{2,1,0:T(4,128)(2,1)S(1)}, bf16[1,4,128]{2,1,0:T(4...) all-reduce(bf16[1,512]{1,0:T(2,128)(2,1)S(1)} %convert_element_type, ...), channel_id=1, replica_groups=mesh['rep'=16,'shard'=2] {'rep'}, use_global_device_ids=true, to_apply=%region_28.29 | all-reduce | flops 23728 | bytes 94912 | tf_op jit(solution)/shard_map/psum | solution.py:167
  322.3 2.3 fusion.86
  324.6 59.4 %all-reduce.32.cloned.1.call-done = (bf16[1,1024,1024]{2,1,0:T(8,128)(2,1)}, bf16[1,1024,128]{2,1,0:T(8,128)(2,1)}, bf16[1,1024,1024]{2,1,0:T(8,128)(2,1)}) async-done(((bf16[1,1024,1024]{2,1,0:T(8,128)(2,1)}, bf16[1,1024,128]{2,1,0:T(8,128)(2,1)}, bf16[1,1024,1024]{2,1,0:T(8,128)(2,1)}), (bf16[1,1024,1024]{2,1,0:T(8,128)(2,1)}, bf16[1,1024,128]{2,1,0:T(8,128)(2,1)}, ...) | async-done | bytes 4456464 | tf_op jit(solution)/shard_map/psum | solution.py:169
  384.0 4.2 convert_element_type.313
  389.1 2.5 convert_element_type.345
  391.5 162.4 %all-gather.3.cloned.1.call-done = bf16[16384,1024]{1,0:T(8,128)(2,1)} async-done(((bf16[1024,1024]{1,0:T(8,128)(2,1)}), bf16[16384,1024]{1,0:T(8,128)(2,1)}) %all-gather.3.cloned.1.call-update) | async-done | bytes 33554448 | tf_op jit(solution)/shard_map/all_gather | solution.py:14
  553.9 13.2 %reduce.4 = bf16[1024,1024]{1,0:T(8,128)(2,1)} reduce(bf16[16,1024,1024]{2,1,0:T(8,128)(2,1)} %bitcast.248, bf16[]{:T(256)} %constant.145.clone.1), dimensions={0}, to_apply=%region_29.30 | reduce | flops 15728640 | bytes 35651584 | tf_op jit(solution)/shard_map/reduce_sum | solution.py:15
  567.2 4.1 bitcast_convert_fusion
  (369 shorter events, 97.9 us)
Async XLA Ops:
  7.2 104.6 %copy-start = (bf16[1,1024,1024]{2,1,0:T(8,128)(2,1)S(1)}, bf16[1,1024,1024]{2,1,0:T(8,128)(2,1)}, u32[]{:S(2)}) copy-start(bf16[1,1024,1024]{2,1,0:T(8,128)(2,1)} %param.26) | copy-start | bytes 6291460
  7.2 220.3 %reduce-scatter.13.cloned.1.call-start = ((), (), s32[]{:S(2)}) async-start(), calls=%async_computation.7 | async-start | bytes 196608
  11.4 45.7 %copy-start.48 = (f32[256]{0:T(256)}, f32[256]{0:T(256)S(1)}, u32[]{:S(2)}) copy-start(f32[256]{0:T(256)S(1)} %get-tuple-element.414) | copy-start | bytes 3076
  11.4 45.7 %copy-start.50 = (f32[256]{0:T(256)}, f32[256]{0:T(256)S(1)}, u32[]{:S(2)}) copy-start(f32[256]{0:T(256)S(1)} %get-tuple-element.415) | copy-start | bytes 3076
  11.4 45.7 %copy-start.52 = (f32[256]{0:T(256)}, f32[256]{0:T(256)S(1)}, u32[]{:S(2)}) copy-start(f32[256]{0:T(256)S(1)} %get-tuple-element.416) | copy-start | bytes 3076
  19.6 12.1 %copy-start.81 = (f32[1,1024]{1,0:T(1,128)S(1)}, f32[1,1024]{1,0:T(1,128)}, u32[]{:S(2)}) copy-start(f32[1,1024]{1,0:T(1,128)} %param.32) | copy-start | bytes 12292
  28.4 5.5 copy-start.54
  28.4 5.5 copy-start.56
  28.4 5.4 copy-start.58
  28.4 5.4 copy-start.60
  39.7 8.6 %copy-start.86 = (f32[1,4,128]{2,1,0:T(4,128)S(1)}, f32[1,4,128]{2,1,0:T(4,128)}, u32[]{:S(2)}) copy-start(f32[1,4,128]{2,1,0:T(4,128)} %param.31) | copy-start | bytes 6148
  39.7 12.9 %copy-start.95 = (f32[1,128]{1,0:T(1,128)S(1)}, f32[1,128]{1,0:T(1,128)}, u32[]{:S(2)}) copy-start(f32[1,128]{1,0:T(1,128)} %param.33) | copy-start | bytes 1540
  39.7 18.3 %copy-start.96 = (f32[1,16]{1,0:T(1,128)S(1)}, f32[1,16]{1,0:T(1,128)}, u32[]{:S(2)}) copy-start(f32[1,16]{1,0:T(1,128)} %param.35) | copy-start | bytes 196
  39.7 18.3 %copy-start.7 = (bf16[256,1024]{1,0:T(8,128)(2,1)S(1)}, bf16[256,1024]{1,0:T(8,128)(2,1)}, u32[]{:S(2)}) copy-start(bf16[256,1024]{1,0:T(8,128)(2,1)} %copy-done.6) | copy-start | bytes 1572868
  39.7 18.3 %copy-start.42 = (bf16[1,1024,16]{1,2,0:T(8,128)(2,1)S(1)}, bf16[1,1024,16]{1,2,0:T(8,128)(2,1)}, u32[]{:S(2)}) copy-start(bf16[1,1024,16]{1,2,0:T(8,128)(2,1)} %param.29) | copy-start | bytes 98308
  39.8 18.3 %copy-start.87 = (f32[1,16]{1,0:T(1,128)S(1)}, f32[1,16]{1,0:T(1,128)}, u32[]{:S(2)}) copy-start(f32[1,16]{1,0:T(1,128)} %param.34) | copy-start | bytes 196
  48.3 10.6 %copy-start.26 = (f32[256,256]{1,0:T(8,128)}, f32[256,256]{1,0:T(8,128)S(1)}, u32[]{:S(2)}) copy-start(f32[256,256]{1,0:T(8,128)S(1)} %fusion.90) | copy-start | bytes 786436
  52.6 5.4 copy-start.68
  52.6 8.3 %copy-start.70 = (f32[1,1,256]{2,1,0:T(1,128)}, f32[1,1,256]{2,1,0:T(1,128)S(1)}, u32[]{:S(2)}) copy-start(f32[1,1,256]{2,1,0:T(1,128)S(1)} %get-tuple-element.411) | copy-start | bytes 3076
  52.6 8.3 %copy-start.72 = (f32[1,1,256]{2,1,0:T(1,128)}, f32[1,1,256]{2,1,0:T(1,128)S(1)}, u32[]{:S(2)}) copy-start(f32[1,1,256]{2,1,0:T(1,128)S(1)} %get-tuple-element.412) | copy-start | bytes 3076
  52.6 8.3 %copy-start.74 = (f32[1,1,256]{2,1,0:T(1,128)}, f32[1,1,256]{2,1,0:T(1,128)S(1)}, u32[]{:S(2)}) copy-start(f32[1,1,256]{2,1,0:T(1,128)S(1)} %get-tuple-element.413) | copy-start | bytes 3076
  58.0 5.5 copy-start.84
  60.9 9.0 %copy-start.46 = (f32[4,64]{1,0:T(4,128)}, f32[4,64]{1,0:T(4,128)S(1)}, u32[]{:S(2)}) copy-start(f32[4,64]{1,0:T(4,128)S(1)} %get-tuple-element.409) | copy-start | bytes 3076
  99.6 6.3 %copy-start.33 = (f32[4,64,64]{2,1,0:T(8,128)}, f32[4,64,64]{2,1,0:T(8,128)S(1)}, u32[]{:S(2)}) copy-start(f32[4,64,64]{2,1,0:T(8,128)S(1)} %fusion.132) | copy-start | bytes 196612
  111.8 19.3 %copy-start.44 = (f32[1,1024]{1,0:T(1,128)S(1)}, f32[1,1024]{1,0:T(1,128)}, u32[]{:S(2)}) copy-start(f32[1,1024]{1,0:T(1,128)} %param.37) | copy-start | bytes 12292
  122.9 8.1 %copy-start.82 = (f32[128]{0:T(128)}, f32[128]{0:T(128)S(1)}, u32[]{:S(2)}) copy-start(f32[128]{0:T(128)S(1)} %convert_element_type.296) | copy-start | bytes 1540
  153.3 7.3 %copy-start.2 = (f32[4,64,16,64]{1,3,2,0:T(8,128)S(1)}, f32[4,64,16,64]{1,3,2,0:T(8,128)}, u32[]{:S(2)}) copy-start(f32[4,64,16,64]{1,3,2,0:T(8,128)} %copy.211) | copy-start | bytes 3145732
  190.0 6.0 %copy-start.36 = (f32[4,64,64]{2,1,0:T(8,128)S(1)}, f32[4,64,64]{2,1,0:T(8,128)}, u32[]{:S(2)}) copy-start(f32[4,64,64]{2,1,0:T(8,128)} %get-tuple-element.305) | copy-start | bytes 196612
  190.0 6.4 %copy-start.35 = (f32[4,64,128]{2,1,0:T(8,128)S(1)}, f32[4,64,128]{2,1,0:T(8,128)}, u32[]{:S(2)}) copy-start(f32[4,64,128]{2,1,0:T(8,128)} %fusion.49) | copy-start | bytes 393220
  190.0 6.6 %copy-start.27 = (f32[256,256]{1,0:T(8,128)S(1)}, f32[256,256]{1,0:T(8,128)}, u32[]{:S(2)}) copy-start(f32[256,256]{1,0:T(8,128)} %copy-done.26) | copy-start | bytes 786436
  190.0 6.7 %copy-start.31 = (f32[256,256]{1,0:T(8,128)S(1)}, f32[256,256]{1,0:T(8,128)}, u32[]{:S(2)}) copy-start(f32[256,256]{1,0:T(8,128)} %get-tuple-element.380) | copy-start | bytes 786436
  190.1 6.7 %copy-start.49 = (f32[256]{0:T(256)S(1)}, f32[256]{0:T(256)}, u32[]{:S(2)}) copy-start(f32[256]{0:T(256)} %copy-done.48) | copy-start | bytes 3076
  190.1 6.7 %copy-start.51 = (f32[256]{0:T(256)S(1)}, f32[256]{0:T(256)}, u32[]{:S(2)}) copy-start(f32[256]{0:T(256)} %copy-done.50) | copy-start | bytes 3076
  190.1 6.7 %copy-start.53 = (f32[256]{0:T(256)S(1)}, f32[256]{0:T(256)}, u32[]{:S(2)}) copy-start(f32[256]{0:T(256)} %copy-done.52) | copy-start | bytes 3076
  198.6 50.9 %reduce-scatter.15.cloned.1.call-start = ((), (), s32[]{:S(2)}) async-start(), calls=%async_computation.8 | async-start | bytes 98304
  199.5 50.9 %reduce-scatter.11.cloned.1.call-start = ((), (), s32[]{:S(2)}) async-start(), calls=%async_computation.5 | async-start | bytes 786432 | tf_op jit(solution)/shard_map/reduce_scatter | solution.py:287
  230.3 92.0 %reduce-scatter.9.cloned.1.call-start = ((), (), s32[]{:S(2)}) async-start(), calls=%async_computation.4 | async-start | bytes 786432 | tf_op jit(solution)/shard_map/reduce_scatter | solution.py:251
  233.6 150.4 %all-reduce.32.cloned.1.call-start = ((), (), s32[]{:S(2)}) async-start(), calls=%async_computation.9 | async-start | bytes 8912896 | tf_op jit(solution)/shard_map/psum | solution.py:169
  239.0 5.1 copy-start.76
  239.0 5.2 copy-start.92
  239.0 314.9 %all-gather.3.cloned.1.call-start = ((), (), s32[]{:S(2)}) async-start(), calls=%async_computation.6 | async-start | bytes 35651584 | tf_op jit(solution)/shard_map/all_gather | solution.py:14
  242.1 7.4 %copy-start.97 = (f32[1,16]{1,0:T(1,128)S(1)}, f32[1,16]{1,0:T(1,128)}, u32[]{:S(2)}) copy-start(f32[1,16]{1,0:T(1,128)} %param.35) | copy-start | bytes 196
  242.1 8.3 %copy-start.24 = (bf16[128,1024]{1,0:T(8,128)(2,1)S(1)}, bf16[128,1024]{1,0:T(8,128)(2,1)}, u32[]{:S(2)}) copy-start(bf16[128,1024]{1,0:T(8,128)(2,1)} %param.23) | copy-start | bytes 786436
  242.1 8.3 %copy-start.80 = (f32[128]{0:T(128)S(1)}, f32[128]{0:T(128)}, u32[]{:S(2)}) copy-start(f32[128]{0:T(128)} %copy-done.79) | copy-start | bytes 1540
  242.1 80.2 %copy-start.91 = (f32[128]{0:T(128)S(1)}, f32[128]{0:T(128)}, u32[]{:S(2)}) copy-start(f32[128]{0:T(128)} %copy-done.90) | copy-start | bytes 1540
  242.1 80.2 %copy-start.32 = (bf16[128,1024]{1,0:T(8,128)(2,1)S(1)}, bf16[128,1024]{1,0:T(8,128)(2,1)}, u32[]{:S(2)}) copy-start(bf16[128,1024]{1,0:T(8,128)(2,1)} %param.24) | copy-start | bytes 786436
  242.1 80.2 %copy-start.83 = (f32[128]{0:T(128)S(1)}, f32[128]{0:T(128)}, u32[]{:S(2)}) copy-start(f32[128]{0:T(128)} %copy-done.82) | copy-start | bytes 1540
  553.9 17.3 %copy-start.1 = (bf16[1,1024,1024]{2,1,0:T(8,128)(2,1)S(1)}, bf16[1,1024,1024]{2,1,0:T(8,128)(2,1)}, u32[]{:S(2)}) copy-start(bf16[1,1024,1024]{2,1,0:T(8,128)(2,1)} %param.26) | copy-start | bytes 6291460
  (57 other events, 145.9 us)
Sparse Core Ops, SparseCore 0:
  198.7 11.7 reduce-scatter.12
  213.3 9.8 reduce-scatter.14
  230.4 16.0 reduce-scatter.10
  249.3 14.6 reduce-scatter.8
  269.0 114.9 all-reduce.31
  386.0 167.8 all-gather.2
